TPU v7x, 32 devices: a whole 2x2x4 slice. The times are simulated.
32 devices in a mesh: parts: 2 (over x), dp: 4 (over y, core), shard: 4 (over z).
Axes of the slice: x: 2, y: 2, z: 4, core: 2. Of those that a mesh axis runs over, the one named last changes fastest.
Arguments:
- projected: bfloat16 [7680, 7680], P(('parts', 'dp', 'shard')), parts along dimension 0, may hold values from -4 to 4
- residual: bfloat16 [7680, 2560], P(('parts', 'dp', 'shard')), parts along dimension 0, may hold values from -6 to 6
- out_weight: bfloat16 [2560, 2560], P(None, 'shard'), may hold values from -0.125 to 0.125
- probe_weight: bfloat16 [2, 2560, 8], replicated, may hold values from -0.125 to 0.125
- labels: int32 [7680], P(('parts', 'dp', 'shard')), parts along dimension 0, may hold values from 0 to 7
- lengths: int32 [32, 9], P(('parts', 'dp', 'shard')), parts along dimension 0, may hold values from 12 to 48, as said below
- destination: int32 [32, 9], P(('parts', 'dp', 'shard')), parts along dimension 0, may hold values from 0 to 3, as said below
Outputs:
- hidden_rows: bfloat16 [18432, 2560], P(('parts', 'dp', 'shard')), parts along dimension 0
- probe_grad: float32 [4, 2560, 8], P('parts'), parts along dimension 0
There are 2 independent parts, one for each index of `parts`. A program takes and returns all parts, laid end to end along the dimension named above; an argument that names none is the same for every part. Nothing has to cross between parts.
Inputs may be any that keep to these rules, and one draw needn't show every extreme that they name: Each row of lengths sums to 240 and holds exactly one protein of length 48. `destination`: A loader assigns at most 3 proteins to any one dp index; in every shard column one dp index is assigned exactly 3 proteins by every loader of that column.
All inputs are finite; a program needn't handle non-finite values.
Results may differ from a plain program's by a relative error of at most 0.0031.
Values may be sent and summed in bfloat16 or wider, within the bound.
No kernel may reach another device: no remote copies, remote signals or barrier semaphores. Data moves between devices by JAX's collectives and lax.ppermute only.
A program may use at most 128 MiB of HBM per device.

v0:
```python
import jax
import jax.numpy as jnp
from jax import lax
from jax.sharding import PartitionSpec as P

HS = 128
CLASSES = 8
LMAX = 48
TOK_DEV = 240


def attend(blocks, block_lengths):
    block_count = blocks.shape[0]
    span_rows = blocks.shape[1]
    head_width = blocks.shape[2] // 3
    head_count = head_width // HS
    queries = blocks[:, :, :head_width].reshape(block_count, span_rows, head_count, HS)
    key_rows = blocks[:, :, head_width : 2 * head_width].reshape(
        block_count, span_rows, head_count, HS
    )
    value_rows = blocks[:, :, 2 * head_width :].reshape(block_count, span_rows, head_count, HS)
    scores = jnp.einsum(
        "plhs,pmhs->phlm", queries, key_rows, preferred_element_type=jnp.float32
    ) * HS ** (-0.5)
    keep_mask = (jnp.arange(span_rows, dtype=jnp.int32)[None, :] < block_lengths[:, None]).astype(
        jnp.float32
    )
    weights = jnp.exp(scores) * keep_mask[:, None, None, :]
    denominator = (
        jnp.sum(weights, axis=-1, keepdims=True)
        + (block_lengths == 0).astype(jnp.float32)[:, None, None, None]
    )
    weight_low = (weights / denominator).astype(jnp.bfloat16)
    attended = jnp.einsum(
        "phlm,pmhs->plhs", weight_low, value_rows, preferred_element_type=jnp.float32
    )
    return attended.reshape(block_count * span_rows, head_width).astype(jnp.bfloat16)


def project(attended, out_weight):
    return jnp.dot(
        attended,
        lax.all_gather(out_weight, "shard", axis=1, tiled=True),
        preferred_element_type=jnp.float32,
    )


def probe_terms(represent_x, represent_h, label_rows, keep_mask, probe_weight):
    one_hot = (label_rows[:, None] == jnp.arange(CLASSES, dtype=jnp.int32)[None, :]).astype(
        jnp.float32
    )
    collected = []
    for which, represent in enumerate((represent_x, represent_h)):
        logits = jnp.dot(represent, probe_weight[which], preferred_element_type=jnp.float32)
        exponent = jnp.exp(logits)
        likelihood = exponent / jnp.sum(exponent, axis=1, keepdims=True)
        mismatch = ((likelihood - one_hot) * keep_mask[:, None] / TOK_DEV).astype(jnp.bfloat16)
        collected.append(
            lax.dot_general(
                represent, mismatch, (((0,), (0,)), ((), ())), preferred_element_type=jnp.float32
            )
        )
    return jnp.stack(collected)


def per_device(projected, residual, out_weight, probe_weight, labels, lengths, destination):
    group_size = lax.axis_size("dp")
    prot_count = lengths.shape[1]
    slot_count = -(-prot_count // group_size)
    tok_count = projected.shape[0]
    lens_own = lengths[0]
    dest_own = destination[0]
    starts = jnp.cumsum(lens_own) - lens_own
    offsets = jnp.arange(LMAX, dtype=jnp.int32)
    positions = jnp.arange(prot_count, dtype=jnp.int32)
    same_dest = dest_own[:, None] == dest_own[None, :]
    earlier = positions[:, None] > positions[None, :]
    slot_rank = jnp.sum((same_dest & earlier).astype(jnp.int32), axis=1)
    slot_match = (
        dest_own[None, None, :] == jnp.arange(group_size, dtype=jnp.int32)[:, None, None]
    ) & (slot_rank[None, None, :] == jnp.arange(slot_count, dtype=jnp.int32)[None, :, None])
    match_int = slot_match.astype(jnp.int32)
    slot_start = jnp.sum(match_int * starts, axis=2)
    slot_len = jnp.sum(match_int * lens_own, axis=2)
    block_count = group_size * slot_count
    row_index = jnp.minimum(slot_start[:, :, None] + offsets, tok_count - 1).reshape(
        group_size, slot_count * LMAX
    )
    live_rows = (offsets[None, None, :] < slot_len[:, :, None]).reshape(
        group_size, slot_count * LMAX
    )
    rows_send = jnp.where(live_rows[:, :, None], jnp.take(projected, row_index, axis=0), 0)
    resid_send = jnp.where(live_rows[:, :, None], jnp.take(residual, row_index, axis=0), 0)
    label_send = jnp.where(live_rows, jnp.take(labels, row_index), 0)
    got_labels, got_lengths = (
        lax.all_to_all(label_send, "dp", split_axis=0, concat_axis=0, tiled=True),
        lax.all_to_all(slot_len, "dp", split_axis=0, concat_axis=0, tiled=True),
    )
    got_rows, got_resid = (
        lax.all_to_all(rows_send, "dp", split_axis=0, concat_axis=0, tiled=True),
        lax.all_to_all(resid_send, "dp", split_axis=0, concat_axis=0, tiled=True),
    )
    lengths_recv = got_lengths.reshape(block_count)
    attended = attend(got_rows.reshape(block_count, LMAX, -1), lengths_recv)
    keep_mask = (offsets[None, :] < lengths_recv[:, None]).astype(jnp.float32).reshape(-1)
    represent = got_resid.reshape(block_count * LMAX, -1)
    mixed_rows = project(attended, out_weight) + represent.astype(jnp.float32)
    hidden = (mixed_rows * keep_mask[:, None]).astype(jnp.bfloat16)
    grad_terms = probe_terms(represent, hidden, got_labels.reshape(-1), keep_mask, probe_weight)
    grad_sum = lax.psum(grad_terms, ("dp", "shard"))
    return (hidden, grad_sum)


def solution(mesh):
    return jax.shard_map(
        per_device,
        mesh=mesh,
        in_specs=(
            P(("parts", "dp", "shard"), None),
            P(("parts", "dp", "shard"), None),
            P(None, "shard"),
            P(),
            P(("parts", "dp", "shard")),
            P(("parts", "dp", "shard"), None),
            P(("parts", "dp", "shard"), None),
        ),
        out_specs=(P(("parts", "dp", "shard"), None), P("parts", None, None)),
        check_vma=False,
    )
```

profile of v0, /device:TPU:8, one launch (start us, length us, event | category | flops | bytes accessed | tf_op | source)
XLA Modules:
  0.0 349.7 jit_solution(5877579920904036037)
XLA Ops:
  7.2 0.7 all-gather.2.cloned.1.call-update
  7.9 0.2 reduce-window.8
  8.1 0.2 convert_reduce_fusion
  8.3 0.2 fusion.37
  8.5 0.7 copy.27
  9.2 3.2 all-to-all-start.1
  12.4 0.1 copy.22
  12.5 0.1 copy.23
  12.7 0.1 add.97
  12.8 0.1 add.101
  12.8 0.1 add.108
  13.0 0.1 lt.134
  13.1 0.1 lt.146
  13.2 0.1 lt.131
  13.3 0.1 reshape.363
  13.4 4.2 %gather_fusion.1 = bf16[576,2560]{1,0:T(8,128)(2,1)} fusion(bf16[240,2560]{1,0:T(8,128)(2,1)S(1)} %copy-done, s32[1024]{0:T(1024)S(1)} %pad_clamp_fusion), kind=kCustom, calls=%fused_computation.1 | custom fusion | bytes 5900544 | tf_op jit(solution)/shard_map/jit(_take)/gather | solution.py:93
  17.6 3.9 %gather_fusion.2 = s32[576]{0:T(1024)S(1)} fusion(s32[240]{0:T(256)S(1)} %copy-done.2, s32[1024]{0:T(1024)S(1)} %pad_clamp_fusion), kind=kCustom, calls=%fused_computation.2 | custom fusion | bytes 6912 | tf_op jit(solution)/shard_map/jit(_take)/gather | solution.py:94
  21.5 0.1 gather.17
  21.6 0.6 copy.31
  22.3 3.3 all-to-all-start.3
  25.5 4.2 %select_select_fusion.1 = bf16[4,144,2560]{2,1,0:T(8,128)(2,1)} fusion(bf16[4,144,2560]{2,1,0:T(8,128)(2,1)} %bitcast.61, pred[4,144]{1,0:T(4,128)(4,1)S(1)} %get-tuple-element.8, pred[4,144]{1,0:T(4,128)(4,1)S(1)} %get-tuple-element.7), kind=kLoop, calls=%fused_computation.23 | loop fusion | flops 2949120 | bytes 5899392 | tf_op jit(solution)/shard_map/jit(_where)/select_n | solution.py:93
  29.7 22.4 %gather_fusion = bf16[576,7680]{1,0:T(8,128)(2,1)} fusion(bf16[240,7680]{1,0:T(8,128)(2,1)} %param.7, s32[1024]{0:T(1024)S(1)} %pad_clamp_fusion), kind=kCustom, calls=%fused_computation | custom fusion | bytes 17697024 | tf_op jit(solution)/shard_map/jit(_take)/gather | solution.py:92
  52.1 4.6 %all-to-all-start.2 = ((bf16[4,144,2560]{2,1,0:T(8,128)(2,1)}), bf16[4,144,2560]{2,1,0:T(8,128)(2,1)}, u32[]{:S(2)}, u32[]{:S(2)}) async-start(bf16[4,144,2560]{2,1,0:T(8,128)(2,1)} %select_select_fusion.1), calls=%async_computation.2 | async-start | bytes 5898240 | tf_op jit(solution)/shard_map/all_to_all | solution.py:101
  56.8 8.1 %select_select_fusion = bf16[4,144,7680]{2,1,0:T(8,128)(2,1)} fusion(bf16[4,144,7680]{2,1,0:T(8,128)(2,1)} %bitcast.60, pred[4,144]{1,0:T(4,128)(4,1)S(1)} %get-tuple-element.8, pred[4,144]{1,0:T(4,128)(4,1)S(1)} %get-tuple-element.7), kind=kLoop, calls=%fused_computation.3 | loop fusion | flops 8847360 | bytes 17695872 | tf_op jit(solution)/shard_map/jit(_where)/select_n | solution.py:92
  64.9 26.7 %all-to-all-done.2 = bf16[4,144,2560]{2,1,0:T(8,128)(2,1)} async-done(((bf16[4,144,2560]{2,1,0:T(8,128)(2,1)}), bf16[4,144,2560]{2,1,0:T(8,128)(2,1)}, u32[]{:S(2)}, u32[]{:S(2)}) %all-to-all-start.2) | async-done | bytes 2949152 | tf_op jit(solution)/shard_map/all_to_all | solution.py:101
  91.6 5.7 %all-to-all-start = ((bf16[4,144,7680]{2,1,0:T(8,128)(2,1)}), bf16[4,144,7680]{2,1,0:T(8,128)(2,1)}, u32[]{:S(2)}, u32[]{:S(2)}) async-start(bf16[4,144,7680]{2,1,0:T(8,128)(2,1)} %select_select_fusion), calls=%async_computation | async-start | bytes 17694720 | tf_op jit(solution)/shard_map/all_to_all | solution.py:100
  97.3 0.2 all-reduce.2.cloned.1.call-start
  97.6 0.5 broadcast.237
  98.1 0.7 reduce.4
  98.7 0.1 lt.142
  98.9 0.1 reshape.360
  99.0 0.1 eq.84
  99.1 2.7 fusion.43
  101.8 2.3 convolution_bitcast_fusion.1
  104.1 91.3 %all-to-all-done = bf16[4,144,7680]{2,1,0:T(8,128)(2,1)} async-done(((bf16[4,144,7680]{2,1,0:T(8,128)(2,1)}), bf16[4,144,7680]{2,1,0:T(8,128)(2,1)}, u32[]{:S(2)}, u32[]{:S(2)}) %all-to-all-start) | async-done | bytes 8847392 | tf_op jit(solution)/shard_map/all_to_all | solution.py:100
  195.4 4.0 %slice_bitcast_fusion.2 = (bf16[12,6,20,8,128]{4,3,2,1,0:T(8,128)(2,1)S(1)}, bf16[12,6,20,8,128]{4,3,2,1,0:T(8,128)(2,1)S(1)}, bf16[12,6,20,8,128]{4,3,2,1,0:T(8,128)(2,1)S(1)}) fusion(bf16[12,48,7680]{2,1,0:T(8,128)(2,1)} %bitcast.5), kind=kLoop, calls=%fused_computation.22 | loop fusion | bytes 17694720
  199.4 1.7 fusion
  201.1 0.1 broadcast_add_fusion
  201.2 2.0 convert_bitcast_fusion
  203.2 2.6 copy.30
  205.8 28.8 %all-gather.2.cloned.1.call-done = bf16[2560,2560]{1,0:T(8,128)(2,1)} async-done(((bf16[2560,640]{1,0:T(8,128)(2,1)}), bf16[2560,2560]{1,0:T(8,128)(2,1)}) %all-gather.2.cloned.1.call-update) | async-done | bytes 13107216 | tf_op jit(solution)/shard_map/all_gather | solution.py:43
  234.6 12.4 %multiply_convert_fusion = bf16[576,2560]{1,0:T(8,128)(2,1)S(1)} fusion(bf16[576,2560]{1,0:T(8,128)(2,1)} %bitcast.9, bf16[2560,2560]{1,0:T(8,128)(2,1)} %all-gather.2.cloned.1.call-done, bf16[72,8,20,128]{3,2,1,0:T(8,128)(2,1)} %bitcast.62, f32[576]{0:T(1024)S(1)} %reshape.360), kind=kOutput, calls=%fused_computation.4 | convolution fusion | flops 7555645440 | bytes 21956864 | tf_op jit(solution)/shard_map/dot_general | solution.py:41
  246.9 0.9 fusion.42
  247.8 0.5 convolution_bitcast_fusion
  248.3 0.2 copy-done.3
  248.5 0.7 pad_maximum_fusion
  249.2 92.0 %all-reduce.2.cloned.1.call-done = f32[2,2560,8]{1,2,0:T(8,128)} async-done(((f32[2,2560,8]{1,2,0:T(8,128)}), f32[2,2560,8]{1,2,0:T(8,128)}) %all-reduce.2.cloned.1.call-update) | async-done | bytes 163856 | tf_op jit(solution)/shard_map/psum | solution.py:110
  341.3 1.6 copy.62
  (30 shorter events, 0.4 us)
Async XLA Ops:
  7.2 6.2 %copy-start = (bf16[240,2560]{1,0:T(8,128)(2,1)S(1)}, bf16[240,2560]{1,0:T(8,128)(2,1)}, u32[]{:S(2)}) copy-start(bf16[240,2560]{1,0:T(8,128)(2,1)} %param.8) | copy-start | bytes 3686404
  7.2 0.8 copy-start.5
  7.2 0.9 copy-start.6
  7.2 227.4 %all-gather.2.cloned.1.call-start = ((), (), s32[]{:S(2)}) async-start(), calls=%async_computation.4 | async-start | bytes 16384000 | tf_op jit(solution)/shard_map/all_gather | solution.py:43
  9.2 13.1 %all-to-all-start.1 = ((s32[4,1,3]{2,1,0:T(1,128)}), s32[4,1,3]{2,1,0:T(1,128)S(1)}, u32[]{:S(2)}, u32[]{:S(2)}) async-start(s32[4,1,3]{2,1,0:T(1,128)} %copy.27), calls=%async_computation.1 | async-start | bytes 4096 | tf_op jit(solution)/shard_map/all_to_all | solution.py:97
  13.4 4.2 %copy-start.2 = (s32[240]{0:T(256)S(1)}, s32[240]{0:T(256)}, u32[]{:S(2)}) copy-start(s32[240]{0:T(256)} %param.11) | copy-start | bytes 2884
  22.3 29.9 %all-to-all-start.3 = ((s32[4,1,144]{2,1,0:T(1,128)}), s32[4,1,144]{2,1,0:T(1,128)S(1)}, u32[]{:S(2)}, u32[]{:S(2)}) async-start(s32[4,1,144]{2,1,0:T(1,128)} %copy.31), calls=%async_computation.3 | async-start | bytes 8192 | tf_op jit(solution)/shard_map/all_to_all | solution.py:96
  52.1 39.5 %all-to-all-start.2 = ((bf16[4,144,2560]{2,1,0:T(8,128)(2,1)}), bf16[4,144,2560]{2,1,0:T(8,128)(2,1)}, u32[]{:S(2)}, u32[]{:S(2)}) async-start(bf16[4,144,2560]{2,1,0:T(8,128)(2,1)} %select_select_fusion.1), calls=%async_computation.2 | async-start | bytes 5898240 | tf_op jit(solution)/shard_map/all_to_all | solution.py:101
  64.9 34.2 %copy-start.4 = (bf16[2,2560,8]{1,2,0:T(8,128)(2,1)S(1)}, bf16[2,2560,8]{1,2,0:T(8,128)(2,1)}, u32[]{:S(2)}) copy-start(bf16[2,2560,8]{1,2,0:T(8,128)(2,1)} %param.10) | copy-start | bytes 245764
  91.6 103.8 %all-to-all-start = ((bf16[4,144,7680]{2,1,0:T(8,128)(2,1)}), bf16[4,144,7680]{2,1,0:T(8,128)(2,1)}, u32[]{:S(2)}, u32[]{:S(2)}) async-start(bf16[4,144,7680]{2,1,0:T(8,128)(2,1)} %select_select_fusion), calls=%async_computation | async-start | bytes 17694720 | tf_op jit(solution)/shard_map/all_to_all | solution.py:100
  97.3 244.0 %all-reduce.2.cloned.1.call-start = ((), (), s32[]{:S(2)}) async-start(), calls=%async_computation.5 | async-start | bytes 327680 | tf_op jit(solution)/shard_map/psum | solution.py:110
  246.9 1.6 copy-start.3
  247.8 95.0 %copy-start.1 = (bf16[240,2560]{1,0:T(8,128)(2,1)S(1)}, bf16[240,2560]{1,0:T(8,128)(2,1)}, u32[]{:S(2)}) copy-start(bf16[240,2560]{1,0:T(8,128)(2,1)} %param.8) | copy-start | bytes 3686404
Sparse Core Ops, SparseCore 0:
  9.6 224.9 all-gather.1
  249.4 91.8 all-reduce.1
where the time goes:
time: 350 us
  waiting for transfers between devices  239 us (68%)
  local copies, waits for them, and re-layouts  42 us (12%)
  matrix products  22.5 us (6%)
  starting transfers between devices  17 us (5%)
  other arithmetic  14.4 us (4%)
  between operations  14.3 us (4%)
    psum x1, waiting for transfers between devices, per_device(): grad_sum = lax.psum(grad_terms, ('dp', 'shard'))  92 us
    all_to_all x1, waiting for transfers between devices, per_device(): lax.all_to_all(rows_send, 'dp', split_axis=0, concat_axis=0, tiled=True)  91.3 us
    all_gather x1, waiting for transfers between devices, project(): lax.all_gather(out_weight, 'shard', axis=1, tiled=True)  28.8 us
    all_to_all x1, waiting for transfers between devices, per_device(): lax.all_to_all(resid_send, 'dp', split_axis=0, concat_axis=0, tiled=True)  26.7 us
    gather x1, local copies, waits for them, and re-layouts, per_device(): jnp.take(projected, row_index, axis=0)  22.4 us
    dot_general x1, matrix products, project(): jnp.dot(attended, lax.all_gather(out_weight, 'shard', axis=1, tiled=True)...  12.4 us
    select_n x1, other arithmetic, per_device(): jnp.where(live_rows[:, :, None], jnp.take(projected, row_index, axis=0), 0)  8.14 us
  transfers between devices with their start and end apart: 6, of which 4 were waited for; matrix products, arithmetic and copies ran while one was open for 18% of the time, Pallas kernels for 0%

commit v1 on v0

--- a/solution.py
+++ b/solution.py
@@ -107,7 +107,7 @@
     mixed_rows = project(attended, out_weight) + represent.astype(jnp.float32)
     hidden = (mixed_rows * keep_mask[:, None]).astype(jnp.bfloat16)
     grad_terms = probe_terms(represent, hidden, got_labels.reshape(-1), keep_mask, probe_weight)
-    grad_sum = lax.psum(grad_terms, ("dp", "shard"))
+    grad_sum = lax.psum(lax.psum(grad_terms, "dp"), "shard")
     return (hidden, grad_sum)
 
 

time: 350 us -> 330 us (0.943)
  waiting for transfers between devices: 239 us -> 218 us
    psum x1 -> x2, waiting for transfers between devices: 92 us -> 70.2 us  [per_device(): grad_sum = lax.psum(lax.psum(grad_terms, 'dp'), 'shard')]
  transfers between devices with their start and end apart: 6 -> 7, of which waited for: 4 -> 5; matrix products, arithmetic and copies ran while one was open for 18% -> 19% of each run, Pallas kernels for 0% -> 0%
where the time goes in v1:
time: 330 us; the launch traced here: 328 us
  waiting for transfers between devices  218 us (66%)
  local copies, waits for them, and re-layouts  42 us (13%)
  matrix products  22.5 us (7%)
  starting transfers between devices  17.1 us (5%)
  other arithmetic  14.4 us (4%)
  between operations  14 us (4%)
    all_to_all x1, waiting for transfers between devices, per_device(): lax.all_to_all(rows_send, 'dp', split_axis=0, concat_axis=0, tiled=True)  91.3 us
    psum x2, waiting for transfers between devices, per_device(): grad_sum = lax.psum(lax.psum(grad_terms, 'dp'), 'shard')  70.2 us
    all_gather x1, waiting for transfers between devices, project(): lax.all_gather(out_weight, 'shard', axis=1, tiled=True)  28.8 us
    all_to_all x1, waiting for transfers between devices, per_device(): lax.all_to_all(resid_send, 'dp', split_axis=0, concat_axis=0, tiled=True)  26.7 us
    gather x1, local copies, waits for them, and re-layouts, per_device(): jnp.take(projected, row_index, axis=0)  22.4 us
    dot_general x1, matrix products, project(): jnp.dot(attended, lax.all_gather(out_weight, 'shard', axis=1, tiled=True)...  12.4 us
    select_n x1, other arithmetic, per_device(): jnp.where(live_rows[:, :, None], jnp.take(projected, row_index, axis=0), 0)  8.14 us
  transfers between devices with their start and end apart: 7, of which 5 were waited for; matrix products, arithmetic and copies ran while one was open for 19% of the time, Pallas kernels for 0%

profile of v1, /device:TPU:8, one launch (start us, length us, event | category | flops | bytes accessed | tf_op | source)
XLA Modules:
  0.0 327.6 jit_solution(5709629040614551625)
XLA Ops:
  7.2 0.7 all-gather.2.cloned.1.call-update
  7.9 0.2 reduce-window.8
  8.1 0.2 convert_reduce_fusion
  8.3 0.2 fusion.37
  8.5 0.7 copy.27
  9.2 3.2 all-to-all-start.1
  12.4 0.1 copy.22
  12.5 0.1 copy.23
  12.7 0.1 add.99
  12.8 0.1 add.103
  12.8 0.1 add.110
  13.0 0.1 lt.134
  13.1 0.1 lt.146
  13.2 0.1 lt.131
  13.3 0.1 reshape.363
  13.4 4.2 %gather_fusion.1 = bf16[576,2560]{1,0:T(8,128)(2,1)} fusion(bf16[240,2560]{1,0:T(8,128)(2,1)S(1)} %copy-done, s32[1024]{0:T(1024)S(1)} %pad_clamp_fusion), kind=kCustom, calls=%fused_computation.1 | custom fusion | bytes 5900544 | tf_op jit(solution)/shard_map/jit(_take)/gather | solution.py:93
  17.6 3.9 %gather_fusion.2 = s32[576]{0:T(1024)S(1)} fusion(s32[240]{0:T(256)S(1)} %copy-done.2, s32[1024]{0:T(1024)S(1)} %pad_clamp_fusion), kind=kCustom, calls=%fused_computation.2 | custom fusion | bytes 6912 | tf_op jit(solution)/shard_map/jit(_take)/gather | solution.py:94
  21.5 0.1 gather.17
  21.6 0.6 copy.31
  22.3 3.3 all-to-all-start.3
  25.5 4.2 %select_select_fusion.1 = bf16[4,144,2560]{2,1,0:T(8,128)(2,1)} fusion(bf16[4,144,2560]{2,1,0:T(8,128)(2,1)} %bitcast.61, pred[4,144]{1,0:T(4,128)(4,1)S(1)} %get-tuple-element.8, pred[4,144]{1,0:T(4,128)(4,1)S(1)} %get-tuple-element.7), kind=kLoop, calls=%fused_computation.23 | loop fusion | flops 2949120 | bytes 5899392 | tf_op jit(solution)/shard_map/jit(_where)/select_n | solution.py:93
  29.7 22.4 %gather_fusion = bf16[576,7680]{1,0:T(8,128)(2,1)} fusion(bf16[240,7680]{1,0:T(8,128)(2,1)} %param.7, s32[1024]{0:T(1024)S(1)} %pad_clamp_fusion), kind=kCustom, calls=%fused_computation | custom fusion | bytes 17697024 | tf_op jit(solution)/shard_map/jit(_take)/gather | solution.py:92
  52.1 4.6 %all-to-all-start.2 = ((bf16[4,144,2560]{2,1,0:T(8,128)(2,1)}), bf16[4,144,2560]{2,1,0:T(8,128)(2,1)}, u32[]{:S(2)}, u32[]{:S(2)}) async-start(bf16[4,144,2560]{2,1,0:T(8,128)(2,1)} %select_select_fusion.1), calls=%async_computation.2 | async-start | bytes 5898240 | tf_op jit(solution)/shard_map/all_to_all | solution.py:101
  56.8 8.1 %select_select_fusion = bf16[4,144,7680]{2,1,0:T(8,128)(2,1)} fusion(bf16[4,144,7680]{2,1,0:T(8,128)(2,1)} %bitcast.60, pred[4,144]{1,0:T(4,128)(4,1)S(1)} %get-tuple-element.8, pred[4,144]{1,0:T(4,128)(4,1)S(1)} %get-tuple-element.7), kind=kLoop, calls=%fused_computation.3 | loop fusion | flops 8847360 | bytes 17695872 | tf_op jit(solution)/shard_map/jit(_where)/select_n | solution.py:92
  64.9 26.7 %all-to-all-done.2 = bf16[4,144,2560]{2,1,0:T(8,128)(2,1)} async-done(((bf16[4,144,2560]{2,1,0:T(8,128)(2,1)}), bf16[4,144,2560]{2,1,0:T(8,128)(2,1)}, u32[]{:S(2)}, u32[]{:S(2)}) %all-to-all-start.2) | async-done | bytes 2949152 | tf_op jit(solution)/shard_map/all_to_all | solution.py:101
  91.6 5.7 %all-to-all-start = ((bf16[4,144,7680]{2,1,0:T(8,128)(2,1)}), bf16[4,144,7680]{2,1,0:T(8,128)(2,1)}, u32[]{:S(2)}, u32[]{:S(2)}) async-start(bf16[4,144,7680]{2,1,0:T(8,128)(2,1)} %select_select_fusion), calls=%async_computation | async-start | bytes 17694720 | tf_op jit(solution)/shard_map/all_to_all | solution.py:100
  97.3 0.2 all-reduce.3.cloned.1.call-start
  97.6 0.5 broadcast.237
  98.1 0.7 reduce.4
  98.7 0.1 lt.142
  99.0 0.1 eq.84
  99.1 2.7 fusion.43
  101.8 2.3 convolution_bitcast_fusion.1
  104.1 91.3 %all-to-all-done = bf16[4,144,7680]{2,1,0:T(8,128)(2,1)} async-done(((bf16[4,144,7680]{2,1,0:T(8,128)(2,1)}), bf16[4,144,7680]{2,1,0:T(8,128)(2,1)}, u32[]{:S(2)}, u32[]{:S(2)}) %all-to-all-start) | async-done | bytes 8847392 | tf_op jit(solution)/shard_map/all_to_all | solution.py:100
  195.4 4.0 %slice_bitcast_fusion.2 = (bf16[12,6,20,8,128]{4,3,2,1,0:T(8,128)(2,1)S(1)}, bf16[12,6,20,8,128]{4,3,2,1,0:T(8,128)(2,1)S(1)}, bf16[12,6,20,8,128]{4,3,2,1,0:T(8,128)(2,1)S(1)}) fusion(bf16[12,48,7680]{2,1,0:T(8,128)(2,1)} %bitcast.5), kind=kLoop, calls=%fused_computation.22 | loop fusion | bytes 17694720
  199.4 1.7 fusion
  201.1 0.1 broadcast_add_fusion
  201.2 2.0 convert_bitcast_fusion
  203.2 2.6 copy.30
  205.8 28.8 %all-gather.2.cloned.1.call-done = bf16[2560,2560]{1,0:T(8,128)(2,1)} async-done(((bf16[2560,640]{1,0:T(8,128)(2,1)}), bf16[2560,2560]{1,0:T(8,128)(2,1)}) %all-gather.2.cloned.1.call-update) | async-done | bytes 13107216 | tf_op jit(solution)/shard_map/all_gather | solution.py:43
  234.6 12.4 %multiply_convert_fusion = bf16[576,2560]{1,0:T(8,128)(2,1)S(1)} fusion(bf16[576,2560]{1,0:T(8,128)(2,1)} %bitcast.9, bf16[2560,2560]{1,0:T(8,128)(2,1)} %all-gather.2.cloned.1.call-done, bf16[72,8,20,128]{3,2,1,0:T(8,128)(2,1)} %bitcast.62, f32[576]{0:T(1024)S(1)} %reshape.360), kind=kOutput, calls=%fused_computation.4 | convolution fusion | flops 7555645440 | bytes 21956864 | tf_op jit(solution)/shard_map/dot_general | solution.py:41
  246.9 0.9 fusion.42
  247.8 0.5 convolution_bitcast_fusion
  248.3 0.2 copy-done.3
  248.5 0.7 pad_maximum_fusion
  249.3 33.1 %all-reduce.3.cloned.1.call-done = f32[2,2560,8]{1,2,0:T(8,128)} async-done(((f32[2,2560,8]{1,2,0:T(8,128)}), f32[2,2560,8]{1,2,0:T(8,128)}) %all-reduce.3.cloned.1.call-update) | async-done | bytes 163856 | tf_op jit(solution)/shard_map/psum | solution.py:110
  282.5 37.1 %all-reduce.5.cloned.1.call-done = f32[2,2560,8]{1,2,0:T(8,128)} async-done(((f32[2,2560,8]{1,2,0:T(8,128)}), f32[2,2560,8]{1,2,0:T(8,128)}) %all-reduce.5.cloned.1.call-update) | async-done | bytes 163856 | tf_op jit(solution)/shard_map/psum | solution.py:110
  319.5 1.6 copy.63
  (33 shorter events, 0.5 us)
Async XLA Ops:
  7.2 6.2 %copy-start = (bf16[240,2560]{1,0:T(8,128)(2,1)S(1)}, bf16[240,2560]{1,0:T(8,128)(2,1)}, u32[]{:S(2)}) copy-start(bf16[240,2560]{1,0:T(8,128)(2,1)} %param.8) | copy-start | bytes 3686404
  7.2 0.8 copy-start.5
  7.2 0.9 copy-start.6
  7.2 227.4 %all-gather.2.cloned.1.call-start = ((), (), s32[]{:S(2)}) async-start(), calls=%async_computation.4 | async-start | bytes 16384000 | tf_op jit(solution)/shard_map/all_gather | solution.py:43
  9.2 13.1 %all-to-all-start.1 = ((s32[4,1,3]{2,1,0:T(1,128)}), s32[4,1,3]{2,1,0:T(1,128)S(1)}, u32[]{:S(2)}, u32[]{:S(2)}) async-start(s32[4,1,3]{2,1,0:T(1,128)} %copy.27), calls=%async_computation.1 | async-start | bytes 4096 | tf_op jit(solution)/shard_map/all_to_all | solution.py:97
  13.4 4.2 %copy-start.2 = (s32[240]{0:T(256)S(1)}, s32[240]{0:T(256)}, u32[]{:S(2)}) copy-start(s32[240]{0:T(256)} %param.11) | copy-start | bytes 2884
  22.3 29.9 %all-to-all-start.3 = ((s32[4,1,144]{2,1,0:T(1,128)}), s32[4,1,144]{2,1,0:T(1,128)S(1)}, u32[]{:S(2)}, u32[]{:S(2)}) async-start(s32[4,1,144]{2,1,0:T(1,128)} %copy.31), calls=%async_computation.3 | async-start | bytes 8192 | tf_op jit(solution)/shard_map/all_to_all | solution.py:96
  52.1 39.5 %all-to-all-start.2 = ((bf16[4,144,2560]{2,1,0:T(8,128)(2,1)}), bf16[4,144,2560]{2,1,0:T(8,128)(2,1)}, u32[]{:S(2)}, u32[]{:S(2)}) async-start(bf16[4,144,2560]{2,1,0:T(8,128)(2,1)} %select_select_fusion.1), calls=%async_computation.2 | async-start | bytes 5898240 | tf_op jit(solution)/shard_map/all_to_all | solution.py:101
  64.9 34.2 %copy-start.4 = (bf16[2,2560,8]{1,2,0:T(8,128)(2,1)S(1)}, bf16[2,2560,8]{1,2,0:T(8,128)(2,1)}, u32[]{:S(2)}) copy-start(bf16[2,2560,8]{1,2,0:T(8,128)(2,1)} %param.10) | copy-start | bytes 245764
  91.6 103.8 %all-to-all-start = ((bf16[4,144,7680]{2,1,0:T(8,128)(2,1)}), bf16[4,144,7680]{2,1,0:T(8,128)(2,1)}, u32[]{:S(2)}, u32[]{:S(2)}) async-start(bf16[4,144,7680]{2,1,0:T(8,128)(2,1)} %select_select_fusion), calls=%async_computation | async-start | bytes 17694720 | tf_op jit(solution)/shard_map/all_to_all | solution.py:100
  97.3 185.1 %all-reduce.3.cloned.1.call-start = ((), (), s32[]{:S(2)}) async-start(), calls=%async_computation.5 | async-start | bytes 327680 | tf_op jit(solution)/shard_map/psum | solution.py:110
  246.9 1.6 copy-start.3
  247.8 73.3 %copy-start.1 = (bf16[240,2560]{1,0:T(8,128)(2,1)S(1)}, bf16[240,2560]{1,0:T(8,128)(2,1)}, u32[]{:S(2)}) copy-start(bf16[240,2560]{1,0:T(8,128)(2,1)} %param.8) | copy-start | bytes 3686404
  249.2 70.3 %all-reduce.5.cloned.1.call-start = ((), (), s32[]{:S(2)}) async-start(), calls=%async_computation.6 | async-start | bytes 327680 | tf_op jit(solution)/shard_map/psum | solution.py:110
Sparse Core Ops, SparseCore 0:
  9.6 224.9 all-gather.1
  249.4 33.0 all-reduce.2
  284.8 34.7 all-reduce.4
